TPU v7x, 32 devices: a whole 2x2x4 slice. The times are simulated.
32 devices in a mesh: groups: 2 (over x), src: 8 (over z, y), tile: 2 (over core).
Axes of the slice: x: 2, y: 2, z: 4, core: 2. Of those that a mesh axis runs over, the one named last changes fastest.
Arguments:
- mask: float32 [2048, 1024], P(('groups', 'tile')), parts along dimension 0, may hold values from 0 to 1
- target: float32 [2048, 1024], P(('groups', 'tile')), parts along dimension 0, may hold values from 0 to 1
- pupil: float32 [64, 64], replicated, may hold values from 0.1 to 1.9
- source_shift: int32 [24, 2], replicated, may hold values from -24 to 24
- source_weight: float32 [24], replicated, may hold values from 0.25 to 4
Outputs:
- mask_gradient: float32 [2048, 1024], P(('groups', 'tile'), 'src'), parts along dimension 0
There are 2 independent parts, one for each index of `groups`. A program takes and returns all parts, laid end to end along the dimension named above; an argument that names none is the same for every part. Nothing has to cross between parts.
Inputs may be any that keep to these rules, and one draw needn't show every extreme that they name: `source_shift`: integer frequency shifts of the source points.
All inputs are finite; a program needn't handle non-finite values.
Results may differ from a plain program's by a relative error of at most 0.0003.
Values sent between devices are 32-bit elements; how exact they have to be, the bound alone decides.
A program may use at most 128 MiB of HBM per device.

v0:
```python
import functools

import numpy as np

import jax
import jax.numpy as jnp
from jax import lax
from jax.experimental import pallas as pl
from jax.experimental.pallas import tpu as pltpu
from jax.sharding import PartitionSpec as P

TS = 512
HALO = 64
PAD = 640
GRID = 128
REACH = 24
CHUNK = 256

MESH = pl.DeviceIdType.MESH
f32, bf16 = jnp.float32, jnp.bfloat16
resist_gain = 25.0
resist_level = 0.25


def tables(freqs, columns):
    pixels = np.arange(PAD)[:, None]
    samples = np.arange(GRID)[None, :] * (PAD // GRID)
    spread = np.ones((PAD, GRID))
    for p in range(1, GRID // 2):
        spread += 2.0 * np.cos(2.0 * np.pi * (p * (pixels - samples) % PAD) / PAD)
    spread /= GRID
    tiles = columns // TS
    across = np.zeros((columns, tiles * GRID))
    for c in range(tiles):
        low, high = max(0, c * TS - HALO), min(columns, c * TS - HALO + PAD)
        across[low:high, c * GRID : (c + 1) * GRID] = spread[low + HALO - c * TS : high + HALO - c * TS]
    bins = np.arange(-freqs // 2 - REACH, freqs // 2 + REACH)[:, None] * np.arange(GRID)[None, :]
    angle = 2.0 * np.pi * (bins % GRID) / GRID
    waves = np.concatenate([np.cos(angle), np.sin(angle)], axis=1)
    return spread, across, waves


def rotation(waves, freqs):
    centre = waves[REACH : REACH + freqs]
    cosine, sine = centre[:, :GRID].T, centre[:, GRID:].T
    return np.block([[cosine, -sine], [sine, cosine]])


def two(array):
    high = array.astype(np.float32).astype(bf16)
    low = (array - high.astype(np.float64)).astype(bf16)
    return np.stack([high, low])


def split(x):
    high = x.astype(bf16)
    return high, (x - high.astype(f32)).astype(bf16)


NN = (((1,), (0,)), ((), ()))
NT = (((1,), (1,)), ((), ()))


def mm(a, b, dims=NN):
    def part(x, y):
        return lax.dot_general(x, y, dims, preferred_element_type=f32)

    return part(a[0], b[0]) + (part(a[0], b[1]) + part(a[1], b[0]))


def pair(ref, *index):
    return ref[(0, *index)], ref[(1, *index)]


def resist_slope(intensity, target):
    printed = jax.nn.sigmoid(resist_gain * (intensity - resist_level))
    return 2.0 * (printed - target) * resist_gain * printed * (1.0 - printed)


def halves(y, count, freqs):
    real, imag = [], []
    for c in range(count):
        top = y[2 * c * freqs : (2 * c + 1) * freqs]
        low = y[(2 * c + 1) * freqs : (2 * c + 2) * freqs]
        real.append(top[:, :GRID] - low[:, GRID:])
        imag.append(top[:, GRID:] + low[:, :GRID])
    return real, imag


def each(count, body):
    if count <= 16:
        for i in range(count):
            body(i)
    else:
        lax.fori_loop(0, count, lambda i, c: (body(i), c)[1], 0)


def kernel(
    n, own, freqs, tiles,
    mask_any, target_any, pupil_ref, shift_ref, weight_ref,
    core_any, coret_any, across_any, waves_any, fixed_any, turn_any, turnt_any, edge_any, edget_any,
    out_ref,
    core_ref, coret_ref, across_ref, waves_ref, fixed_ref, turn_ref, turnt_ref, edge_ref, edget_ref,
    mask_ref, target_ref, halo_ref, shifted_ref, low_ref, field_ref, up_ref, pull_ref,
    part_ref, gather_ref, total_ref, rim_ref, rimin_ref,
    load_sem, halo_sem, rim_sem, send_sem, recv_sem,
):
    me = lax.axis_index("src")
    side = lax.axis_index("tile")
    owners = part_ref.shape[1]
    held = part_ref.shape[2]
    width = out_ref.shape[1]

    barrier = pltpu.get_barrier_semaphore()
    pl.semaphore_signal(barrier, inc=1, device_id={"tile": 1 - side}, device_id_type=MESH)

    def greet(i):
        pl.semaphore_signal(barrier, inc=1, device_id={"src": lax.rem(me + i + 1, n)}, device_id_type=MESH)

    each(n - 1, greet)

    places = [
        (waves_any, waves_ref), (mask_any, mask_ref), (coret_any, coret_ref), (across_any, across_ref),
        (edget_any, edget_ref), (fixed_any, fixed_ref), (turn_any, turn_ref), (target_any, target_ref),
        (core_any, core_ref), (turnt_any, turnt_ref), (edge_any, edge_ref),
    ]
    loads = [pltpu.make_async_copy(source, place, load_sem.at[i]) for i, (source, place) in enumerate(places)]
    for load in loads:
        load.start()
    loads[0].wait()

    span = waves_ref.shape[1]
    gap = lax.broadcasted_iota(jnp.int32, (freqs, span), 1) - lax.broadcasted_iota(jnp.int32, (freqs, span), 0)
    for s in range(own):
        for axis in (0, 1):
            picks = jnp.where(gap == shift_ref[axis, me * own + s] + REACH, 1.0, 0.0).astype(bf16)
            shifted_ref[s, axis] = lax.dot_general(picks, waves_ref[0], NN, preferred_element_type=f32) + lax.dot_general(
                picks, waves_ref[1], NN, preferred_element_type=f32
            )

    low_ref[...] = jnp.zeros_like(low_ref)

    def project(left, source, height):
        def block(i, carry):
            at = pl.multiple_of(i * 256, 256)
            rows = mm(left, split(source[0:height, pl.ds(at, 256)]))
            low_ref[...] += mm(split(rows), pair(across_ref, pl.ds(at, 256)))
            return carry

        lax.fori_loop(0, mask_ref.shape[1] // 256, block, 0)

    pl.semaphore_wait(barrier, n)
    first = pl.multiple_of((TS - HALO) * (1 - side), HALO)
    halo = pltpu.make_async_remote_copy(
        src_ref=mask_any.at[pl.ds(first, HALO)],
        dst_ref=halo_ref,
        send_sem=halo_sem.at[0],
        recv_sem=halo_sem.at[1],
        device_id={"tile": 1 - side},
        device_id_type=MESH,
    )
    halo.start()
    for load in loads[1:4]:
        load.wait()
    project(pair(coret_ref), mask_ref, TS)
    for load in loads[4:7]:
        load.wait()
    halo.wait_recv()
    project(pair(edget_ref, side), halo_ref, HALO)

    low = split(low_ref[...])

    def turns():
        return jnp.concatenate(
            [shifted_ref[s, 0, :, half * GRID : (half + 1) * GRID] for s in range(own) for half in (0, 1)], axis=0
        )

    spun = mm(split(turns()), low)
    scaled = pupil_ref[...] * (1.0 / (PAD * PAD))
    scaled = jnp.concatenate([scaled] * (2 * own), axis=0)
    fixed = pair(fixed_ref)

    weights = [weight_ref[me * own + s] for s in range(own)]

    def image(c):
        lanes = slice(c * GRID, (c + 1) * GRID)
        specs = []
        for s in range(own):
            cc = spun[2 * s * freqs : (2 * s + 1) * freqs, lanes]
            ss = spun[(2 * s + 1) * freqs : (2 * s + 2) * freqs, lanes]
            rows = [jnp.concatenate([cc, -ss], axis=1), jnp.concatenate([-ss, -cc], axis=1)]
            specs.append(mm(split(jnp.concatenate(rows, axis=0)), split(shifted_ref[s, 1]), NT))
        spec = jnp.concatenate(specs, axis=0) * scaled
        real, imag = halves(mm(split(spec), fixed), own, freqs)
        stack = jnp.concatenate([jnp.concatenate(real, axis=1), jnp.concatenate(imag, axis=1)], axis=0)
        field = mm(pair(turn_ref), split(stack))
        field_ref[c] = field
        light = jnp.zeros((GRID, GRID), f32)
        for s in range(own):
            re = field[:GRID, s * GRID : (s + 1) * GRID]
            im = field[GRID:, s * GRID : (s + 1) * GRID]
            light = light + weights[s] * (re * re + im * im)
        return light

    def owning_sum(k):
        def owning(condition, action):
            if owners == n:
                action()
            else:
                pl.when(condition)(action)

        def scatter(peer):
            return pltpu.make_async_remote_copy(
                src_ref=part_ref.at[k, lax.rem(peer, owners)],
                dst_ref=gather_ref.at[k, me],
                send_sem=send_sem.at[2 * k, peer],
                recv_sem=recv_sem.at[2 * k, me],
                device_id={"src": peer},
                device_id_type=MESH,
            )

        def arrival(peer):
            return pltpu.make_async_remote_copy(
                src_ref=part_ref.at[k, 0],
                dst_ref=gather_ref.at[k, peer],
                send_sem=send_sem.at[2 * k, peer],
                recv_sem=recv_sem.at[2 * k, peer],
                device_id={"src": peer},
                device_id_type=MESH,
            )

        def share(peer):
            return pltpu.make_async_remote_copy(
                src_ref=total_ref.at[k, lax.rem(me, owners)],
                dst_ref=total_ref.at[k, lax.rem(me, owners)],
                send_sem=send_sem.at[2 * k + 1, peer],
                recv_sem=recv_sem.at[2 * k + 1, me],
                device_id={"src": peer},
                device_id_type=MESH,
            )

        def shared(peer):
            return pltpu.make_async_remote_copy(
                src_ref=total_ref.at[k, lax.rem(peer, owners)],
                dst_ref=total_ref.at[k, lax.rem(peer, owners)],
                send_sem=send_sem.at[2 * k + 1, peer],
                recv_sem=recv_sem.at[2 * k + 1, peer],
                device_id={"src": peer},
                device_id_type=MESH,
            )

        def other(i):
            return lax.rem(me + i + 1, n)

        def begin(value):
            for p in range(owners):
                part_ref[k, p] = value[p * held : (p + 1) * held]
            each(n - 1, lambda i: owning(other(i) < owners, lambda: scatter(other(i)).start()))

        def add_up():
            each(n - 1, lambda i: arrival(other(i)).wait_recv())
            gather_ref[k, me] = part_ref[k, lax.rem(me, owners)]
            block = gather_ref[k, 0]
            if n <= 16:
                for p in range(1, n):
                    block = block + gather_ref[k, p]
            else:
                block = lax.fori_loop(1, n, lambda p, t: t + gather_ref[k, p], block)
            total_ref[k, lax.rem(me, owners)] = block
            each(n - 1, lambda i: share(other(i)).start())

        def middle():
            owning(me < owners, add_up)

        def end():
            each(n - 1, lambda i: owning(other(i) < owners, lambda: shared(other(i)).wait_recv()))
            return jnp.concatenate([total_ref[k, p] for p in range(owners)], axis=0)

        def drain():
            each(n - 1, lambda i: owning(other(i) < owners, lambda: scatter(other(i)).wait_send()))
            owning(me < owners, lambda: each(n - 1, lambda i: share(other(i)).wait_send()))

        return begin, middle, end, drain

    sums = [owning_sum(k) for k in range(2 * tiles)]
    for c in range(tiles):
        sums[c][0](image(c))

    weight = weight_ref[0]
    for s in range(1, n * own):
        weight = weight + weight_ref[s]
    inverse = 1.0 / jnp.full((1, TS), weight, f32)
    for load in loads[7:]:
        load.wait()
    core = pair(core_ref)
    coret = pair(coret_ref)
    lead = split(turns().T)
    for c in range(tiles):
        sums[c][1]()

    def pulled(c, light):
        up_ref[c] = mm(core, split(light))
        pull_ref[c] = jnp.zeros((GRID, GRID), f32)

        def resist(i, carry):
            at = pl.multiple_of(i * CHUNK, CHUNK)
            fine = mm(split(up_ref[c, pl.ds(at, CHUNK), :]), coret)
            slope = resist_slope(fine * inverse, target_ref[pl.ds(at, CHUNK), c * TS : (c + 1) * TS]) * inverse
            rows = mm(split(slope), core)
            pull_ref[c] += mm(pair(coret_ref, slice(None), pl.ds(at, CHUNK)), split(rows))
            return carry

        lax.fori_loop(0, TS // CHUNK, resist, 0)
        return pull_ref[c]

    def gradient(c, pull):
        pull = jnp.concatenate([pull] * 2, axis=0)
        pull = jnp.concatenate([pull * (2.0 * w) for w in weights], axis=1)
        u = mm(pair(turnt_ref), split(field_ref[c] * pull))
        rows = []
        for s in range(own):
            re = u[:freqs, s * GRID : (s + 1) * GRID]
            im = u[freqs:, s * GRID : (s + 1) * GRID]
            rows.append(jnp.concatenate([re, im], axis=1))
            rows.append(jnp.concatenate([im, -re], axis=1))
        back = mm(split(jnp.concatenate(rows, axis=0)), fixed, NT) * scaled
        lows = []
        for s in range(own):
            wide = mm(split(back[2 * s * freqs : 2 * (s + 1) * freqs]), split(shifted_ref[s, 1]))
            real, imag = halves(wide, 1, freqs)
            lows += [real[0], -imag[0]]
        return mm(lead, split(jnp.concatenate(lows, axis=0)))

    for c in range(tiles):
        sums[tiles + c][0](gradient(c, pulled(c, sums[c][2]())))
    for c in range(tiles):
        sums[tiles + c][1]()
    grid_grad = split(jnp.concatenate([sums[tiles + c][2]() for c in range(tiles)], axis=1))
    at = pl.multiple_of(me * width, width)
    block = split(mm(grid_grad, pair(across_ref, pl.ds(at, width)), NT))
    rim_ref[...] = mm(pair(edge_ref, side), block)
    rim = pltpu.make_async_remote_copy(
        src_ref=rim_ref,
        dst_ref=rimin_ref,
        send_sem=rim_sem.at[0],
        recv_sem=rim_sem.at[1],
        device_id={"tile": 1 - side},
        device_id_type=MESH,
    )
    rim.start()
    out_ref[...] = mm(core, block)
    rim.wait_recv()
    out_ref[pl.ds(first, HALO), :] += rimin_ref[...]
    for one in sums:
        one[3]()
    halo.wait_send()
    rim.wait_send()


def shards(mask, target, pupil, source_shift, source_weight):
    n = lax.axis_size("src")
    assert lax.axis_size("tile") == 2
    own = source_shift.shape[0] // n
    freqs = pupil.shape[0]
    columns = mask.shape[1]
    tiles = columns // TS
    width = columns // n
    owners = min(n, GRID // 8)
    spans = tiles * GRID
    spread, across, waves = tables(freqs, columns)
    core = spread[HALO : HALO + TS]
    edges = np.stack([spread[HALO + TS :], spread[:HALO]])
    turn = rotation(waves, freqs)
    constants = [
        two(core), two(core.T), two(across), two(waves),
        two(waves[REACH : REACH + freqs]), two(turn), two(turn.T), two(edges), two(edges.transpose(0, 2, 1)),
    ]
    hbm = pl.BlockSpec(memory_space=pl.ANY)
    vmem = pl.BlockSpec(memory_space=pltpu.VMEM)
    smem = pl.BlockSpec(memory_space=pltpu.SMEM)
    return pl.pallas_call(
        functools.partial(kernel, n, own, freqs, tiles),
        out_shape=jax.ShapeDtypeStruct((TS, width), f32),
        in_specs=[hbm, hbm, vmem, smem, smem] + [hbm] * len(constants),
        out_specs=vmem,
        scratch_shapes=[pltpu.VMEM(c.shape, c.dtype) for c in constants] + [
            pltpu.VMEM((TS, columns), f32),
            pltpu.VMEM((TS, columns), f32),
            pltpu.VMEM((HALO, columns), f32),
            pltpu.VMEM((own, 2, freqs, 2 * GRID), f32),
            pltpu.VMEM((GRID, spans), f32),
            pltpu.VMEM((tiles, 2 * GRID, own * GRID), f32),
            pltpu.VMEM((tiles, TS, GRID), f32),
            pltpu.VMEM((tiles, GRID, GRID), f32),
            pltpu.VMEM((2 * tiles, owners, GRID // owners, GRID), f32),
            pltpu.VMEM((2 * tiles, n, GRID // owners, GRID), f32),
            pltpu.VMEM((2 * tiles, owners, GRID // owners, GRID), f32),
            pltpu.VMEM((HALO, width), f32),
            pltpu.VMEM((HALO, width), f32),
            pltpu.SemaphoreType.DMA((2 + len(constants),)),
            pltpu.SemaphoreType.DMA((2,)),
            pltpu.SemaphoreType.DMA((2,)),
            pltpu.SemaphoreType.DMA((4 * tiles, n)),
            pltpu.SemaphoreType.DMA((4 * tiles, n)),
        ],
        compiler_params=pltpu.CompilerParams(
            collective_id=0, has_side_effects=True, vmem_limit_bytes=60 * 1024 * 1024
        ),
    )(mask, target, pupil, source_shift.T, source_weight, *[jnp.asarray(c) for c in constants])


def solution(mesh):
    placed = (P(("groups", "tile"), None), P(("groups", "tile"), None), P(), P(), P())
    return jax.shard_map(
        shards, mesh=mesh, in_specs=placed, out_specs=P(("groups", "tile"), "src"), check_vma=False
    )
```

profile of v0, /device:TPU:0, one launch (start us, length us, event | category | flops | bytes accessed | tf_op | source)
XLA Modules:
  0.0 42.1 jit_solution(9878127212110628404)
XLA Ops:
  0.0 40.4 %shard_map.136 = f32[512,128]{1,0:T(8,128)} custom-call(f32[512,1024]{1,0:T(8,128)} %mask_any.1, f32[512,1024]{1,0:T(8,128)} %target_any.1, f32[64,64]{1,0:T(8,128)} %pupil_ref.1, s32[2,24]{1,0:T(2,128)} %bitcast.1, f32[24]{0:T(128)} %weight_ref.1, bf16[2,512,128]{2,1,0:T(8,128)(2,1)} %constant.18.clone.core_any, ...), custom_call_target="tpu_custom_call" | custom-call | tf_op jit(solution)/shard_map/pallas_call | solution.py:381
  40.4 1.7 %copy.16 = f32[512,128]{1,0:T(8,128)} copy(f32[512,128]{1,0:T(8,128)} %shard_map.136) | data formatting | bytes 524288
where the time goes:
time: 42.3 us; the launch traced here: 42.1 us
  Pallas kernels  40.4 us (96%)
  local copies, waits for them, and re-layouts  1.67 us (4%)
    pallas_call x1, Pallas kernels, shards(): pl.pallas_call(functools.partial(kernel, n, own, freqs, tiles), out_shape...  40.4 us
    unnamed x1, local copies, waits for them, and re-layouts  1.67 us

commit v1 on v0

v1 whole, which is shorter than its diff:
```python
import functools

import numpy as np

import jax
import jax.numpy as jnp
from jax import lax
from jax.experimental import pallas as pl
from jax.experimental.pallas import tpu as pltpu
from jax.sharding import PartitionSpec as P

TS = 512
HALO = 64
PAD = 640
GRID = 128
REACH = 24
HALF = GRID // 2
CHUNK = 128
BLOCK = 4

MESH = pl.DeviceIdType.MESH
f32, bf16 = jnp.float32, jnp.bfloat16
resist_gain = 25.0
resist_level = 0.25

NN = (((1,), (0,)), ((), ()))
NT = (((1,), (1,)), ((), ()))


def two(array):
    high = array.astype(np.float32).astype(bf16)
    low = (array - high.astype(np.float64)).astype(bf16)
    return np.stack([high, low])


def tables(freqs):
    turn_of = 2.0 * np.pi / PAD
    reach = freqs // 2 + REACH
    frame = np.zeros(GRID)
    frame[: 2 * reach] = np.arange(-reach, reach)
    inside = np.zeros(GRID)
    inside[: 2 * reach] = 1.0

    columns = np.arange(-HALO, PAD + HALO)
    angle = turn_of * ((columns[:, None] * frame[None, :].astype(int)) % PAD)
    valid = ((columns >= 0) & (columns < PAD))[:, None] * inside[None, :]
    across = np.concatenate([np.cos(angle) * valid, np.sin(angle) * valid], axis=1)

    rows = np.arange(PAD)
    k = np.arange(HALF)
    used = (k <= reach)[:, None]
    angle = turn_of * ((k[:, None] * rows[None, :]) % PAD)
    down = np.concatenate([np.cos(angle) * used, -np.sin(angle) * used], axis=0)

    points = np.arange(GRID)
    angle = 2.0 * np.pi / GRID * ((frame[:, None].astype(int) * points[None, :]) % GRID)
    cosine, sine = np.cos(angle) * inside[:, None], np.sin(angle) * inside[:, None]
    wave = np.block([[cosine, sine], [-sine, cosine]])

    centre = np.arange(-freqs // 2, freqs // 2)
    angle = 2.0 * np.pi / GRID * ((points[:, None] * centre[None, :]) % GRID)
    turn = np.block([[np.cos(angle), -np.sin(angle)], [np.sin(angle), np.cos(angle)]])

    samples = points * (PAD // GRID)
    spread = np.ones((PAD, GRID))
    for p in range(1, GRID // 2):
        spread += 2.0 * np.cos(2.0 * np.pi * (p * (rows[:, None] - samples[None, :]) % PAD) / PAD)
    core = (spread / GRID)[HALO : HALO + TS]
    return across, down, wave, turn, core


def split(x):
    high = x.astype(bf16)
    return high, (x - high.astype(f32)).astype(bf16)


def dot(a, b, dims=NN):
    return lax.dot_general(a, b, dims, preferred_element_type=f32)


def mm(a, b, dims=NN):
    return dot(a[0], b[0], dims) + (dot(a[0], b[1], dims) + dot(a[1], b[0], dims))


def pair(ref, *index):
    return ref[(0, *index)], ref[(1, *index)]


def each(count, body):
    if count <= 8:
        for i in range(count):
            body(i)
    else:
        lax.fori_loop(0, count, lambda i, c: (body(i), c)[1], 0)


def at(i, size):
    start = i * size
    return pl.ds(start if isinstance(start, int) else pl.multiple_of(start, size), size)


def kernel(
    n, tiles, sources, freqs, overlap, hop,
    mask_any, target_any, pupil_ref, shift_ref, weight_ref,
    across_any, down_any, downt_any, near_any, neart_any, wave_any, wavet_any, turn_any, turnt_any, core_any, coret_any,
    out_ref,
    across_ref, down_ref, downt_ref, near_ref, neart_ref, wave_ref, wavet_ref, turn_ref, turnt_ref, core_ref, coret_ref,
    mask_ref, target_ref, halo_ref, lens_ref, pick_ref, place_ref, field_ref, light_ref, pull_ref, back_ref,
    own_ref, other_ref, give_ref, side_ref, corner_ref,
    load_sem, halo_sem, own_sem, give_sem, side_sem,
):
    me = lax.axis_index("src")
    side = lax.axis_index("tile")
    per = n // tiles
    c = me // per
    width = out_ref.shape[1]
    counted = HALO // overlap
    edge = me - per
    lefts = (edge >= -counted) & (edge < 0)
    rights = (edge >= 0) & (edge < counted)
    needs = lefts | rights
    source = jnp.where(edge < 0, me + hop, me - hop)
    gives = ((edge - hop >= -counted) & (edge - hop < 0)) | ((edge + hop >= 0) & (edge + hop < counted))
    taker = jnp.where(edge < 0, me + hop, me - hop)

    barrier = pltpu.get_barrier_semaphore()
    side_ref[...] = jnp.zeros_like(side_ref)
    corner_ref[...] = jnp.zeros_like(corner_ref)
    pl.semaphore_signal(barrier, inc=1, device_id={"tile": 1 - side}, device_id_type=MESH)

    @pl.when(needs)
    def _():
        for core in (0, 1):
            pl.semaphore_signal(barrier, inc=1, device_id={"src": source, "tile": core}, device_id_type=MESH)

    first = pl.multiple_of((TS - HALO) * (1 - side), HALO)
    start = pl.multiple_of(c * (mask_any.shape[1] - PAD), GRID)
    begin = pl.multiple_of(c * TS, GRID)
    places = [
        (mask_any.at[:, pl.ds(start, PAD)], mask_ref), (down_any, down_ref), (near_any.at[side], near_ref),
        (across_any.at[:, pl.ds(pl.multiple_of((1 - c) * 2 * HALO, GRID), PAD)], across_ref),
        (wave_any, wave_ref), (turn_any, turn_ref), (core_any, core_ref), (coret_any, coret_ref),
        (target_any.at[:, pl.ds(begin, TS)], target_ref), (turnt_any, turnt_ref), (wavet_any, wavet_ref),
        (downt_any, downt_ref), (neart_any.at[1 - side], neart_ref),
    ]
    loads = [pltpu.make_async_copy(a, b, load_sem.at[i]) for i, (a, b) in enumerate(places)]
    for load in loads:
        load.start()

    scaled = jnp.concatenate([pupil_ref[...] * (1.0 / (PAD * PAD)), jnp.zeros((freqs, GRID - freqs), f32)], axis=1)

    def lens(s):
        lens_ref[at(s, freqs)] = pltpu.roll(scaled, shift_ref[1, s] + REACH, axis=1)
        w = lax.broadcasted_iota(jnp.int32, (freqs, GRID), 0) + (shift_ref[0, s] - freqs // 2)
        lane = lax.broadcasted_iota(jnp.int32, (freqs, GRID), 1)
        cosine = (lane == jnp.abs(w)).astype(f32)
        sine = ((lane - HALF == w) & (w > 0)).astype(f32) - ((lane - HALF == -w) & (w < 0)).astype(f32)
        both = (cosine + sine).astype(bf16)
        pick_ref[at(s, freqs)] = jnp.concatenate([both, both], axis=1)

    each(sources, lens)

    group = GRID // freqs

    def places_of(i):
        lane = lax.broadcasted_iota(jnp.int32, (GRID, GRID), 1)
        row = lax.broadcasted_iota(jnp.int32, (GRID, GRID), 0)
        w = lane - freqs // 2 + shift_ref[0, i * group]
        for g in range(1, group):
            w = jnp.where(lane >= g * freqs, lane - g * freqs - freqs // 2 + shift_ref[0, i * group + g], w)
        cosine = (row == jnp.abs(w)).astype(f32)
        sine = ((row - HALF == w) & (w > 0)).astype(f32) - ((row - HALF == -w) & (w < 0)).astype(f32)
        place_ref[:, at(i, GRID)] = (cosine + sine).astype(bf16)

    each(sources // group, places_of)

    weight = weight_ref[0]
    for s in range(1, sources):
        weight = weight + weight_ref[s]
    inverse = 1.0 / jnp.full((1, GRID), weight, f32)

    pl.semaphore_wait(barrier, 1 + 2 * gives.astype(jnp.int32))
    halo = pltpu.make_async_remote_copy(
        src_ref=mask_any.at[pl.ds(first, HALO), pl.ds(start, PAD)],
        dst_ref=halo_ref,
        send_sem=halo_sem.at[0],
        recv_sem=halo_sem.at[1],
        device_id={"tile": 1 - side},
        device_id_type=MESH,
    )
    halo.start()

    for load in loads[:3]:
        load.wait()
    rows = mm(pair(down_ref), split(mask_ref[...]))
    halo.wait_recv()
    rows = rows + mm(pair(near_ref), split(halo_ref[...]))
    loads[3].wait()
    low = mm(split(rows), pair(across_ref))
    spectrum = split(
        jnp.concatenate(
            [
                jnp.concatenate([low[:HALF, :GRID], -low[:HALF, GRID:]], axis=1),
                jnp.concatenate([low[HALF:, GRID:], low[HALF:, :GRID]], axis=1),
            ],
            axis=0,
        )
    )
    spectrum = jnp.concatenate(spectrum, axis=0)

    for load in loads[4:6]:
        load.wait()
    light_ref[...] = jnp.zeros_like(light_ref)
    wave = pair(wave_ref)
    turn = turn_ref[...]

    def image(i):
        window = dot(pick_ref[at(i, BLOCK * freqs)], spectrum)
        lenses = lens_ref[at(i, BLOCK * freqs)]
        spec = split(window * jnp.concatenate([lenses, lenses], axis=1))
        z = mm(spec, wave)
        stack = jnp.concatenate(
            [
                jnp.concatenate([z[s * freqs : (s + 1) * freqs, :GRID], z[s * freqs : (s + 1) * freqs, GRID:]], axis=0)
                for s in range(BLOCK)
            ],
            axis=1,
        )
        high, less = split(stack)
        field = dot(turn, jnp.concatenate([high, high, less], axis=0))
        field_ref[:, at(i, BLOCK * GRID)] = field
        light = light_ref[...]
        for s in range(BLOCK):
            re = field[:GRID, s * GRID : (s + 1) * GRID]
            im = field[GRID:, s * GRID : (s + 1) * GRID]
            light = light + weight_ref[i * BLOCK + s] * (re * re + im * im)
        light_ref[...] = light

    each(sources // BLOCK, image)

    for load in loads[6:9]:
        load.wait()
    core = pair(core_ref)
    coret = pair(coret_ref)
    up = mm(core, split(light_ref[...] * (resist_gain * inverse)))
    pull = jnp.zeros((GRID, GRID), f32)
    for i in range(TS // CHUNK):
        part = slice(i * CHUNK, (i + 1) * CHUNK)
        fine = mm(split(up[part]), coret)
        decay = jnp.exp(resist_gain * resist_level - fine)
        printed = 1.0 / (1.0 + decay)
        slope = (printed - target_ref[part]) * (decay * printed * printed)
        pull = pull + mm(pair(coret_ref, slice(None), part), split(mm(split(slope), core)))
    pull = pull * (2.0 * resist_gain * inverse)
    pull = jnp.concatenate([pull, pull], axis=0)

    for load in loads[9:]:
        load.wait()
    turnt = pair(turnt_ref)
    wavet = pair(wavet_ref)
    back_ref[...] = jnp.zeros_like(back_ref)

    def gradient(i):
        field = field_ref[:, at(i, BLOCK * GRID)]
        u = mm(turnt, split(field * jnp.concatenate([pull] * BLOCK, axis=1)))
        stack = jnp.concatenate(
            [
                jnp.concatenate([u[:freqs, s * GRID : (s + 1) * GRID], u[freqs:, s * GRID : (s + 1) * GRID]], axis=1)
                for s in range(BLOCK)
            ],
            axis=0,
        )
        z = mm(split(stack), wavet)
        lenses = lens_ref[at(i, BLOCK * freqs)]
        lenses = jnp.concatenate(
            [lenses[s * freqs : (s + 1) * freqs] * (2.0 * weight_ref[i * BLOCK + s]) for s in range(BLOCK)], axis=0
        )
        high, less = split(z * jnp.concatenate([lenses, lenses], axis=1))
        place = place_ref[:, at(i, BLOCK * freqs)]
        back_ref[...] += dot(place, high) + dot(place, less)

    each(sources // BLOCK, gradient)

    back = back_ref[...]
    spectrum = split(
        jnp.concatenate(
            [
                jnp.concatenate([back[:HALF, :GRID], -back[:HALF, GRID:]], axis=1),
                jnp.concatenate([back[HALF:, GRID:], back[HALF:, :GRID]], axis=1),
            ],
            axis=0,
        )
    )

    def columns(first_column, count):
        begin = first_column - start
        return mm(pair(across_ref, pl.ds(pl.multiple_of(begin, count), count)), spectrum, NT)

    def give(core, ref, sem):
        offset = pl.multiple_of(jnp.where(edge < 0, 0, width - overlap), overlap)
        return pltpu.make_async_remote_copy(
            src_ref=give_ref,
            dst_ref=ref.at[pl.ds(offset, overlap)],
            send_sem=give_sem.at[sem],
            recv_sem=side_sem.at[sem],
            device_id={"src": taker, "tile": core},
            device_id_type=MESH,
        )

    def take(ref, sem):
        offset = pl.multiple_of(jnp.where(edge < 0, width - overlap, 0), overlap)
        return pltpu.make_async_remote_copy(
            src_ref=give_ref,
            dst_ref=ref.at[pl.ds(offset, overlap)],
            send_sem=give_sem.at[sem],
            recv_sem=side_sem.at[sem],
            device_id={"src": source, "tile": side},
            device_id_type=MESH,
        )

    @pl.when(gives)
    def _():
        give_ref[...] = columns(taker * width + jnp.where(edge < 0, 0, width - overlap), overlap)
        give(side, side_ref, 0).start()
        give(1 - side, corner_ref, 1).start()

    own = columns(me * width, width)
    own_ref[...] = own
    swap = pltpu.make_async_remote_copy(
        src_ref=own_ref,
        dst_ref=other_ref,
        send_sem=own_sem.at[0],
        recv_sem=own_sem.at[1],
        device_id={"tile": 1 - side},
        device_id_type=MESH,
    )
    swap.start()
    downt = pair(downt_ref)
    out_ref[...] = mm(downt, split(own), NT)
    swap.wait_recv()
    out_ref[pl.ds(first, HALO), :] += mm(pair(neart_ref), split(other_ref[...]), NT)

    @pl.when(needs)
    def _():
        take(side_ref, 0).wait_recv()
        out_ref[...] += mm(downt, split(side_ref[...]), NT)
        take(corner_ref, 1).wait_recv()
        out_ref[pl.ds(first, HALO), :] += mm(pair(neart_ref), split(corner_ref[...]), NT)

    @pl.when(gives)
    def _():
        give(side, side_ref, 0).wait_send()
        give(1 - side, corner_ref, 1).wait_send()

    halo.wait_send()
    swap.wait_send()


def shards(mask, target, pupil, source_shift, source_weight):
    n = lax.axis_size("src")
    assert lax.axis_size("tile") == 2
    sources = source_shift.shape[0]
    freqs = pupil.shape[0]
    columns = mask.shape[1]
    tiles = columns // TS
    assert tiles == 2
    width = columns // n
    overlap = min(width, HALO)
    hop = 1 << ((n.bit_length() - 1) // 2)
    across, down, wave, turn, core = tables(freqs)
    local = down[:, HALO : HALO + TS]
    near = np.stack([down[:, HALO + TS :], down[:, :HALO]])
    turn_two = two(turn)
    constants = [
        two(across), two(local), two(local.T),
        np.stack([two(near[0]), two(near[1])]), np.stack([two(near[0].T), two(near[1].T)]),
        two(wave), two(wave.T), np.concatenate([turn_two[0], turn_two[1], turn_two[0]], axis=1), two(turn.T),
        two(core), two(core.T),
    ]
    scratch = [
        (2, PAD, 2 * GRID), (2, GRID, TS), (2, TS, GRID), (2, GRID, HALO), (2, HALO, GRID),
        (2, 2 * GRID, 2 * GRID), (2, 2 * GRID, 2 * GRID), (2 * GRID, 3 * GRID), (2, GRID, 2 * GRID),
        (2, TS, GRID), (2, GRID, TS),
    ]
    hbm = pl.BlockSpec(memory_space=pl.ANY)
    vmem = pl.BlockSpec(memory_space=pltpu.VMEM)
    smem = pl.BlockSpec(memory_space=pltpu.SMEM)
    return pl.pallas_call(
        functools.partial(kernel, n, tiles, sources, freqs, overlap, hop),
        out_shape=jax.ShapeDtypeStruct((TS, width), f32),
        in_specs=[hbm, hbm, vmem, smem, smem] + [hbm] * len(constants),
        out_specs=vmem,
        scratch_shapes=[pltpu.VMEM(shape, bf16) for shape in scratch] + [
            pltpu.VMEM((TS, PAD), f32),
            pltpu.VMEM((TS, TS), f32),
            pltpu.VMEM((HALO, PAD), f32),
            pltpu.VMEM((sources * freqs, GRID), f32),
            pltpu.VMEM((sources * freqs, 2 * GRID), bf16),
            pltpu.VMEM((GRID, sources * freqs), bf16),
            pltpu.VMEM((2 * GRID, sources * GRID), f32),
            pltpu.VMEM((GRID, GRID), f32),
            pltpu.VMEM((GRID, GRID), f32),
            pltpu.VMEM((GRID, 2 * GRID), f32),
            pltpu.VMEM((width, GRID), f32),
            pltpu.VMEM((width, GRID), f32),
            pltpu.VMEM((overlap, GRID), f32),
            pltpu.VMEM((width, GRID), f32),
            pltpu.VMEM((width, GRID), f32),
            pltpu.SemaphoreType.DMA((2 + len(constants),)),
            pltpu.SemaphoreType.DMA((2,)),
            pltpu.SemaphoreType.DMA((2,)),
            pltpu.SemaphoreType.DMA((2,)),
            pltpu.SemaphoreType.DMA((2,)),
        ],
        compiler_params=pltpu.CompilerParams(
            collective_id=0, has_side_effects=True, vmem_limit_bytes=60 * 1024 * 1024
        ),
    )(mask, target, pupil, source_shift.T, source_weight, *[jnp.asarray(x) for x in constants])


def solution(mesh):
    placed = (P(("groups", "tile"), None), P(("groups", "tile"), None), P(), P(), P())
    return jax.shard_map(
        shards, mesh=mesh, in_specs=placed, out_specs=P(("groups", "tile"), "src"), check_vma=False
    )
```

time: 42.3 us -> 21.8 us (0.52)
  the two profiles are of different devices: /device:TPU:0 before, /device:TPU:13 now
where the time goes in v1:
time: 21.8 us; the launch traced here: 21.6 us
  Pallas kernels  19.9 us (91%)
  local copies, waits for them, and re-layouts  1.67 us (8%)
    pallas_call x1, Pallas kernels, shards(): pl.pallas_call(functools.partial(kernel, n, tiles, sources, freqs, overla...  19.9 us
    unnamed x1, local copies, waits for them, and re-layouts  1.67 us

profile of v1, /device:TPU:13, one launch (start us, length us, event | category | flops | bytes accessed | tf_op | source)
XLA Modules:
  0.0 21.6 jit_solution(13561255668981085470)
XLA Ops:
  0.0 19.9 %shard_map.154 = f32[512,128]{1,0:T(8,128)} custom-call(f32[512,1024]{1,0:T(8,128)} %mask_any.1, f32[512,1024]{1,0:T(8,128)} %target_any.1, f32[64,64]{1,0:T(8,128)} %pupil_ref.1, s32[2,24]{1,0:T(2,128)} %bitcast.1, f32[24]{0:T(128)} %weight_ref.1, bf16[2,768,256]{2,1,0:T(8,128)(2,1)} %constant.22.clone.across_any, ...), custom_call_target="tpu_custom_call" | custom-call | tf_op jit(solution)/shard_map/pallas_call | solution.py:388
  19.9 1.7 %copy.18 = f32[512,128]{1,0:T(8,128)} copy(f32[512,128]{1,0:T(8,128)} %shard_map.154) | data formatting | bytes 524288

commit v2 on v1

--- a/solution.py
+++ b/solution.py
@@ -16,7 +16,7 @@
 REACH = 24
 HALF = GRID // 2
 CHUNK = 128
-BLOCK = 4
+BLOCK = 24
 
 MESH = pl.DeviceIdType.MESH
 f32, bf16 = jnp.float32, jnp.bfloat16
@@ -66,7 +66,12 @@
     for p in range(1, GRID // 2):
         spread += 2.0 * np.cos(2.0 * np.pi * (p * (rows[:, None] - samples[None, :]) % PAD) / PAD)
     core = (spread / GRID)[HALO : HALO + TS]
-    return across, down, wave, turn, core
+    unpack = np.zeros((GRID, GRID))
+    for i in range(2 * reach):
+        w = i - reach
+        unpack[i, abs(w)] = 1.0
+        unpack[i, HALF + abs(w)] = np.sign(w)
+    return across, down, wave, turn, core, unpack
 
 
 def split(x):
@@ -86,8 +91,8 @@
     return ref[(0, *index)], ref[(1, *index)]
 
 
-def each(count, body):
-    if count <= 8:
+def each(count, body, most=BLOCK):
+    if count <= most:
         for i in range(count):
             body(i)
     else:
@@ -102,9 +107,9 @@
 def kernel(
     n, tiles, sources, freqs, overlap, hop,
     mask_any, target_any, pupil_ref, shift_ref, weight_ref,
-    across_any, down_any, downt_any, near_any, neart_any, wave_any, wavet_any, turn_any, turnt_any, core_any, coret_any,
+    unpack_any, repack_any, across_any, down_any, downt_any, near_any, neart_any, wave_any, wavet_any, turn_any, turnt_any, core_any, coret_any,
     out_ref,
-    across_ref, down_ref, downt_ref, near_ref, neart_ref, wave_ref, wavet_ref, turn_ref, turnt_ref, core_ref, coret_ref,
+    unpack_ref, repack_ref, across_ref, down_ref, downt_ref, near_ref, neart_ref, wave_ref, wavet_ref, turn_ref, turnt_ref, core_ref, coret_ref,
     mask_ref, target_ref, halo_ref, lens_ref, pick_ref, place_ref, field_ref, light_ref, pull_ref, back_ref,
     own_ref, other_ref, give_ref, side_ref, corner_ref,
     load_sem, halo_sem, own_sem, give_sem, side_sem,
@@ -137,7 +142,7 @@
     start = pl.multiple_of(c * (mask_any.shape[1] - PAD), GRID)
     begin = pl.multiple_of(c * TS, GRID)
     places = [
-        (mask_any.at[:, pl.ds(start, PAD)], mask_ref), (down_any, down_ref), (near_any.at[side], near_ref),
+        (unpack_any, unpack_ref), (repack_any, repack_ref), (mask_any.at[:, pl.ds(start, PAD)], mask_ref), (down_any, down_ref), (near_any.at[side], near_ref),
         (across_any.at[:, pl.ds(pl.multiple_of((1 - c) * 2 * HALO, GRID), PAD)], across_ref),
         (wave_any, wave_ref), (turn_any, turn_ref), (core_any, core_ref), (coret_any, coret_ref),
         (target_any.at[:, pl.ds(begin, TS)], target_ref), (turnt_any, turnt_ref), (wavet_any, wavet_ref),
@@ -149,28 +154,26 @@
 
     scaled = jnp.concatenate([pupil_ref[...] * (1.0 / (PAD * PAD)), jnp.zeros((freqs, GRID - freqs), f32)], axis=1)
 
+    for load in loads[:2]:
+        load.wait()
+    lane = lax.broadcasted_iota(jnp.int32, (GRID, GRID), 1)
+
     def lens(s):
         lens_ref[at(s, freqs)] = pltpu.roll(scaled, shift_ref[1, s] + REACH, axis=1)
-        w = lax.broadcasted_iota(jnp.int32, (freqs, GRID), 0) + (shift_ref[0, s] - freqs // 2)
-        lane = lax.broadcasted_iota(jnp.int32, (freqs, GRID), 1)
-        cosine = (lane == jnp.abs(w)).astype(f32)
-        sine = ((lane - HALF == w) & (w > 0)).astype(f32) - ((lane - HALF == -w) & (w < 0)).astype(f32)
-        both = (cosine + sine).astype(bf16)
-        pick_ref[at(s, freqs)] = jnp.concatenate([both, both], axis=1)
+        window = unpack_ref[pl.ds(shift_ref[0, s] + REACH, freqs)].astype(bf16)
+        pick_ref[at(s, freqs)] = jnp.concatenate([window, window], axis=1)
 
     each(sources, lens)
 
     group = GRID // freqs
 
     def places_of(i):
-        lane = lax.broadcasted_iota(jnp.int32, (GRID, GRID), 1)
-        row = lax.broadcasted_iota(jnp.int32, (GRID, GRID), 0)
-        w = lane - freqs // 2 + shift_ref[0, i * group]
+        repack = repack_ref[...]
+        place = pltpu.roll(repack, GRID - REACH - shift_ref[0, i * group], axis=1)
         for g in range(1, group):
-            w = jnp.where(lane >= g * freqs, lane - g * freqs - freqs // 2 + shift_ref[0, i * group + g], w)
-        cosine = (row == jnp.abs(w)).astype(f32)
-        sine = ((row - HALF == w) & (w > 0)).astype(f32) - ((row - HALF == -w) & (w < 0)).astype(f32)
-        place_ref[:, at(i, GRID)] = (cosine + sine).astype(bf16)
+            shift = GRID - REACH + g * freqs - shift_ref[0, i * group + g]
+            place = jnp.where(lane >= g * freqs, pltpu.roll(repack, lax.rem(shift, GRID), axis=1), place)
+        place_ref[:, at(i, GRID)] = place.astype(bf16)
 
     each(sources // group, places_of)
 
@@ -190,12 +193,12 @@
     )
     halo.start()
 
-    for load in loads[:3]:
+    for load in loads[2:5]:
         load.wait()
     rows = mm(pair(down_ref), split(mask_ref[...]))
     halo.wait_recv()
     rows = rows + mm(pair(near_ref), split(halo_ref[...]))
-    loads[3].wait()
+    loads[5].wait()
     low = mm(split(rows), pair(across_ref))
     spectrum = split(
         jnp.concatenate(
@@ -208,7 +211,7 @@
     )
     spectrum = jnp.concatenate(spectrum, axis=0)
 
-    for load in loads[4:6]:
+    for load in loads[6:8]:
         load.wait()
     light_ref[...] = jnp.zeros_like(light_ref)
     wave = pair(wave_ref)
@@ -236,9 +239,9 @@
             light = light + weight_ref[i * BLOCK + s] * (re * re + im * im)
         light_ref[...] = light
 
-    each(sources // BLOCK, image)
-
-    for load in loads[6:9]:
+    each(sources // BLOCK, image, 1)
+
+    for load in loads[8:11]:
         load.wait()
     core = pair(core_ref)
     coret = pair(coret_ref)
@@ -254,7 +257,7 @@
     pull = pull * (2.0 * resist_gain * inverse)
     pull = jnp.concatenate([pull, pull], axis=0)
 
-    for load in loads[9:]:
+    for load in loads[11:]:
         load.wait()
     turnt = pair(turnt_ref)
     wavet = pair(wavet_ref)
@@ -279,7 +282,7 @@
         place = place_ref[:, at(i, BLOCK * freqs)]
         back_ref[...] += dot(place, high) + dot(place, less)
 
-    each(sources // BLOCK, gradient)
+    each(sources // BLOCK, gradient, 1)
 
     back = back_ref[...]
     spectrum = split(
@@ -367,12 +370,12 @@
     width = columns // n
     overlap = min(width, HALO)
     hop = 1 << ((n.bit_length() - 1) // 2)
-    across, down, wave, turn, core = tables(freqs)
+    across, down, wave, turn, core, unpack = tables(freqs)
     local = down[:, HALO : HALO + TS]
     near = np.stack([down[:, HALO + TS :], down[:, :HALO]])
     turn_two = two(turn)
     constants = [
-        two(across), two(local), two(local.T),
+        unpack.astype(np.float32), unpack.T.astype(np.float32), two(across), two(local), two(local.T),
         np.stack([two(near[0]), two(near[1])]), np.stack([two(near[0].T), two(near[1].T)]),
         two(wave), two(wave.T), np.concatenate([turn_two[0], turn_two[1], turn_two[0]], axis=1), two(turn.T),
         two(core), two(core.T),
@@ -390,7 +393,7 @@
         out_shape=jax.ShapeDtypeStruct((TS, width), f32),
         in_specs=[hbm, hbm, vmem, smem, smem] + [hbm] * len(constants),
         out_specs=vmem,
-        scratch_shapes=[pltpu.VMEM(shape, bf16) for shape in scratch] + [
+        scratch_shapes=[pltpu.VMEM((GRID, GRID), f32)] * 2 + [pltpu.VMEM(shape, bf16) for shape in scratch] + [
             pltpu.VMEM((TS, PAD), f32),
             pltpu.VMEM((TS, TS), f32),
             pltpu.VMEM((HALO, PAD), f32),

time: 21.8 us -> 19.3 us (0.89)
  Pallas kernels: 19.9 us -> 17.4 us
    pallas_call x1, Pallas kernels: 19.9 us -> 17.4 us  [shards(): pl.pallas_call(functools.partial(kernel, n, tiles, sources, freqs, overla...]
where the time goes in v2:
time: 19.3 us; the launch traced here: 19 us
  Pallas kernels  17.4 us (90%)
  local copies, waits for them, and re-layouts  1.67 us (9%)
    pallas_call x1, Pallas kernels, shards(): pl.pallas_call(functools.partial(kernel, n, tiles, sources, freqs, overla...  17.4 us
    unnamed x1, local copies, waits for them, and re-layouts  1.67 us

profile of v2, /device:TPU:13, one launch (start us, length us, event | category | flops | bytes accessed | tf_op | source)
XLA Modules:
  0.0 19.0 jit_solution(9557895869069142447)
XLA Ops:
  0.0 17.4 %shard_map.172 = f32[512,128]{1,0:T(8,128)} custom-call(f32[512,1024]{1,0:T(8,128)} %mask_any.1, f32[512,1024]{1,0:T(8,128)} %target_any.1, f32[64,64]{1,0:T(8,128)} %pupil_ref.1, s32[2,24]{1,0:T(2,128)} %bitcast.1, f32[24]{0:T(128)} %weight_ref.1, f32[128,128]{1,0:T(8,128)} %constant.26.clone.unpack_any, f32[128,128]{1,0:T(8,128)} %constant.27.clone.repack_any, ...), custom_call_target="tpu_custom_call" | custom-call | tf_op jit(solution)/shard_map/pallas_call | solution.py:391
  17.4 1.7 %copy.20 = f32[512,128]{1,0:T(8,128)} copy(f32[512,128]{1,0:T(8,128)} %shard_map.172) | data formatting | bytes 524288

commit v3 on v2

--- a/solution.py
+++ b/solution.py
@@ -15,7 +15,7 @@
 GRID = 128
 REACH = 24
 HALF = GRID // 2
-CHUNK = 128
+CHUNK = 256
 BLOCK = 24
 
 MESH = pl.DeviceIdType.MESH
@@ -84,7 +84,8 @@
 
 
 def mm(a, b, dims=NN):
-    return dot(a[0], b[0], dims) + (dot(a[0], b[1], dims) + dot(a[1], b[0], dims))
+    axis = dims[0][1][0]
+    return dot(jnp.concatenate([a[0], a[0], a[1]], axis=1), jnp.concatenate([b[0], b[1], b[0]], axis=axis), dims)
 
 
 def pair(ref, *index):

time: 19.3 us -> 18.5 us (0.959)
  Pallas kernels: 17.4 us -> 16.6 us
    pallas_call x1, Pallas kernels: 17.4 us -> 16.6 us  [shards(): pl.pallas_call(functools.partial(kernel, n, tiles, sources, freqs, overla...]
where the time goes in v3:
time: 18.5 us; the launch traced here: 18.3 us
  Pallas kernels  16.6 us (90%)
  local copies, waits for them, and re-layouts  1.67 us (9%)
    pallas_call x1, Pallas kernels, shards(): pl.pallas_call(functools.partial(kernel, n, tiles, sources, freqs, overla...  16.6 us
    unnamed x1, local copies, waits for them, and re-layouts  1.67 us

profile of v3, /device:TPU:13, one launch (start us, length us, event | category | flops | bytes accessed | tf_op | source)
XLA Modules:
  0.0 18.3 jit_solution(907029868893733729)
XLA Ops:
  0.0 16.6 %shard_map.172 = f32[512,128]{1,0:T(8,128)} custom-call(f32[512,1024]{1,0:T(8,128)} %mask_any.1, f32[512,1024]{1,0:T(8,128)} %target_any.1, f32[64,64]{1,0:T(8,128)} %pupil_ref.1, s32[2,24]{1,0:T(2,128)} %bitcast.1, f32[24]{0:T(128)} %weight_ref.1, f32[128,128]{1,0:T(8,128)} %constant.26.clone.unpack_any, f32[128,128]{1,0:T(8,128)} %constant.27.clone.repack_any, ...), custom_call_target="tpu_custom_call" | custom-call | tf_op jit(solution)/shard_map/pallas_call | solution.py:392
  16.6 1.7 %copy.20 = f32[512,128]{1,0:T(8,128)} copy(f32[512,128]{1,0:T(8,128)} %shard_map.172) | data formatting | bytes 524288
